TPU v7x, 32 devices: a whole 2x2x4 slice. The times are simulated.
32 devices in a mesh: grp: 4 (over y, core), dev: 8 (over z, x).
Axes of the slice: x: 2, y: 2, z: 4, core: 2. Of those that a mesh axis runs over, the one named last changes fastest.
Arguments:
- visibilities: bfloat16 [16384, 2, 128], P(('grp', 'dev')), may hold values from -6 to 6
- owner: int32 [16384, 1], P(('grp', 'dev')), may hold values from 0 to 31; in each aligned block of 512 rows (0 to 511, 512 to 1023, ...) at most 32 rows name the same one
- tile_slot: int32 [16384], P(('grp', 'dev')), may hold values from 0 to 511
- kernel_index: int32 [16384, 2], P(('grp', 'dev')), may hold values from 0 to 31
- kernels: bfloat16 [2, 32, 64, 128], replicated, may hold values from -1 to 1
Outputs:
- image: float32 [2, 8192, 8192], P(None, ('grp', 'dev'))
Inputs may be any that keep to these rules, and one draw needn't show every extreme that they name: owner[r, 0] = g * 8 + d names group g and owner d; among the rows of one device no owner is named by more than 32 rows, a bound that some block reaches.
All inputs are finite; a program needn't handle non-finite values.
Results may differ from a plain program's by a relative error of at most 0.0029.
Values may be sent and summed in bfloat16 or wider, within the bound.
A program may use at most 128 MiB of HBM per device.

v0:
```python
import math
import jax
import jax.numpy as jnp
from jax import lax
from jax.sharding import PartitionSpec as P

GRID = 8192
TILE = 64
VIS = 128
QLEN = 128


def complex_product(pattern, left_re, left_im, right_re, right_im):

    def product(first, second):
        return jnp.einsum(pattern, first, second, precision=lax.Precision.HIGHEST)

    return (
        product(left_re, right_re) - product(left_im, right_im),
        product(left_re, right_im) + product(left_im, right_re),
    )


def phase_table(first, second, modulus):
    angle = (
        2.0 * math.pi / modulus * (first[:, None] * second[None, :] % modulus).astype(jnp.float32)
    )
    return (jnp.cos(angle), jnp.sin(angle))


def along_rows(field):
    lines = field.shape[1]
    plen = GRID // QLEN
    outer_idx = jnp.arange(QLEN, dtype=jnp.int32)
    inner_idx = jnp.arange(plen, dtype=jnp.int32)
    outer_re, outer_im = phase_table(outer_idx, outer_idx, QLEN)
    turn_re, turn_im = phase_table(outer_idx, inner_idx, GRID)
    inner_re, inner_im = phase_table(inner_idx, inner_idx, plen)
    field_re = field[0].reshape(lines, QLEN, plen)
    field_im = field[1].reshape(lines, QLEN, plen)
    middle_re, middle_im = complex_product("kq,rqp->rkp", outer_re, outer_im, field_re, field_im)
    middle_re, middle_im = (
        middle_re * turn_re - middle_im * turn_im,
        middle_re * turn_im + middle_im * turn_re,
    )
    result_re, result_im = complex_product("rkp,pb->rbk", middle_re, middle_im, inner_re, inner_im)
    return jnp.stack([result_re.reshape(lines, GRID), result_im.reshape(lines, GRID)])


def along_columns(field, source_order):
    width = field.shape[2]
    plen = GRID // QLEN
    outer_idx = jnp.arange(QLEN, dtype=jnp.int32)
    inner_idx = jnp.arange(plen, dtype=jnp.int32)
    outer_re, outer_im = phase_table(outer_idx, source_order, QLEN)
    turn_re, turn_im = phase_table(outer_idx, inner_idx, GRID)
    inner_re, inner_im = phase_table(inner_idx, inner_idx, plen)
    field_re = field[0].reshape(QLEN, plen, width)
    field_im = field[1].reshape(QLEN, plen, width)
    middle_re, middle_im = complex_product("bk,kpa->bpa", outer_re, outer_im, field_re, field_im)
    turn_re = turn_re[:, :, None]
    turn_im = turn_im[:, :, None]
    middle_re, middle_im = (
        middle_re * turn_re - middle_im * turn_im,
        middle_re * turn_im + middle_im * turn_re,
    )
    result_re, result_im = complex_product("kpa,pb->abk", middle_re, middle_im, inner_re, inner_im)
    scale = 1.0 / GRID
    return jnp.stack(
        [result_re.reshape(width, GRID) * scale, result_im.reshape(width, GRID) * scale]
    )


def local(visibilities, owner, tile_slot, kernel_index, kernels):
    groups = lax.axis_size("grp")
    owners = lax.axis_size("dev")
    devices = groups * owners
    rows_here = visibilities.shape[0]
    capacity = 2 * rows_here // devices
    target = owner[:, 0]
    onehot = (target[:, None] == jnp.arange(devices, dtype=jnp.int32)[None, :]).astype(jnp.int32)
    slot_rank = jnp.sum((jnp.cumsum(onehot, axis=0) - 1) * onehot, axis=1)
    position = target * capacity + slot_rank
    total_rows = devices * capacity
    vis_out = jnp.zeros((total_rows, 2, VIS), jnp.bfloat16).at[position].set(visibilities)
    labels = jnp.concatenate([tile_slot[:, None], kernel_index], axis=1)
    label_out = jnp.zeros((total_rows, 3), jnp.int32).at[position].set(labels)
    vis_in, label_in = (
        lax.all_to_all(
            vis_out.reshape(devices, capacity, 2, VIS),
            ("grp", "dev"),
            split_axis=0,
            concat_axis=0,
            tiled=True,
        ),
        lax.all_to_all(
            label_out.reshape(devices, capacity, 3),
            ("grp", "dev"),
            split_axis=0,
            concat_axis=0,
            tiled=True,
        ),
    )
    vis_in = vis_in.reshape(total_rows, 2, VIS)
    label_in = label_in.reshape(total_rows, 3)
    slab = GRID // devices
    tile_rows = slab // TILE
    tile_cols = GRID // TILE
    block_rows = min(256, total_rows)
    block_count = total_rows // block_rows

    def grid_block(block_index, uv_tiles):
        first_row = block_index * block_rows
        vis_block = lax.dynamic_slice_in_dim(vis_in, first_row, block_rows, 0)
        label_block = lax.dynamic_slice_in_dim(label_in, first_row, block_rows, 0)
        left_kernel = jnp.take(kernels[0], label_block[:, 1], axis=0)
        right_kernel = jnp.take(kernels[1], label_block[:, 2], axis=0)
        weighted = (
            left_kernel.astype(jnp.float32)[:, None, :, :]
            * vis_block.astype(jnp.float32)[:, :, None, :]
        ).astype(jnp.bfloat16)
        terms = jnp.einsum(
            "rcik,rjk->rcij", weighted, right_kernel, preferred_element_type=jnp.float32
        )
        return uv_tiles.at[label_block[:, 0]].add(terms)

    empty = jnp.zeros((tile_rows * tile_cols, 2, TILE, TILE), jnp.float32)
    uv_tiles = lax.fori_loop(0, block_count, grid_block, empty)
    grid_rows = uv_tiles.reshape(tile_rows, tile_cols, 2, TILE, TILE).transpose(2, 0, 3, 1, 4)
    grid_rows = grid_rows.reshape(2, slab, GRID)
    half = along_rows(grid_rows)
    columns = lax.all_to_all(half, ("grp", "dev"), split_axis=2, concat_axis=1, tiled=True)
    source_order = jnp.arange(QLEN, dtype=jnp.int32)
    return along_columns(columns, source_order)


def solution(mesh):
    return jax.shard_map(
        local,
        mesh=mesh,
        in_specs=(
            P(("grp", "dev"), None, None),
            P(("grp", "dev"), None),
            P(("grp", "dev")),
            P(("grp", "dev"), None),
            P(),
        ),
        out_specs=P(None, ("grp", "dev"), None),
        check_vma=False,
    )
```

profile of v0, /device:TPU:0, one launch (start us, length us, event | category | flops | bytes accessed | tf_op | source)
XLA Modules:
  0.0 1191.1 jit_solution(2324823761991537444)
XLA Ops:
  15.5 49.6 %scatter_fusion.1 = bf16[1024,2,128]{2,1,0:T(2,128)(2,1)} fusion(bf16[1024,2,128]{2,1,0:T(2,128)(2,1)} %broadcast_in_dim.29, s32[512]{0:T(512)S(1)} %bitcast.149, bf16[512,2,128]{2,1,0:T(2,128)(2,1)} %param.9), kind=kCustom, calls=%fused_computation.4 | custom fusion | bytes 788480 | tf_op jit(solution)/shard_map/scatter | solution.py:85
  72.4 15.5 %all-to-all-done.1 = bf16[32,32,2,128]{3,2,1,0:T(2,128)(2,1)S(1)} async-done(((bf16[32,32,2,128]{3,2,1,0:T(2,128)(2,1)}), bf16[32,32,2,128]{3,2,1,0:T(2,128)(2,1)S(1)}, u32[]{:S(2)}, u32[]{:S(2)}) %all-to-all-start.1) | async-done | bytes 524320 | tf_op jit(solution)/shard_map/all_to_all | solution.py:89
  99.1 297.3 %while.13 = (s32[]{:T(128)}, f32[512,2,64,64]{3,2,1,0:T(8,128)}, s32[1024,3]{0,1:T(4,128)S(1)}, bf16[2,32,64,128]{3,2,1,0:T(8,128)(2,1)S(1)}, bf16[1024,2,128]{2...) while((s32[]{:T(128)}, f32[512,2,64,64]{3,2,1,0:T(8,128)}, ...), condition=%wide.region_7.9_spmd, body=%wide.region_5.0_spmd.sunk | while | flops 553721088 | bytes 78276800 | solution.py:128
  121.2 52.2 %scatter_fusion = f32[512,2,64,64]{3,2,1,0:T(8,128)} fusion(f32[512,2,64,64]{3,2,1,0:T(8,128)} %get-tuple-element.179, s32[256]{0:T(256)S(1)} %bitcast.141, f32[256,2,64,64]{3,2,1,0:T(8,128)} %fusion.183), kind=kCustom, calls=%fused_computation.2.clone.1 | custom fusion | flops 2097152 | bytes 25166848 | tf_op jit(solution)/shard_map/while/body/eval_jaxpr/scatter-add | solution.py:125
  195.5 52.3 %scatter_fusion = f32[512,2,64,64]{3,2,1,0:T(8,128)} fusion(f32[512,2,64,64]{3,2,1,0:T(8,128)} %get-tuple-element.179, s32[256]{0:T(256)S(1)} %bitcast.141, f32[256,2,64,64]{3,2,1,0:T(8,128)} %fusion.183), kind=kCustom, calls=%fused_computation.2.clone.1 | custom fusion | flops 2097152 | bytes 25166848 | tf_op jit(solution)/shard_map/while/body/eval_jaxpr/scatter-add | solution.py:125
  269.9 52.2 %scatter_fusion = f32[512,2,64,64]{3,2,1,0:T(8,128)} fusion(f32[512,2,64,64]{3,2,1,0:T(8,128)} %get-tuple-element.179, s32[256]{0:T(256)S(1)} %bitcast.141, f32[256,2,64,64]{3,2,1,0:T(8,128)} %fusion.183), kind=kCustom, calls=%fused_computation.2.clone.1 | custom fusion | flops 2097152 | bytes 25166848 | tf_op jit(solution)/shard_map/while/body/eval_jaxpr/scatter-add | solution.py:125
  344.1 52.3 %scatter_fusion = f32[512,2,64,64]{3,2,1,0:T(8,128)} fusion(f32[512,2,64,64]{3,2,1,0:T(8,128)} %get-tuple-element.179, s32[256]{0:T(256)S(1)} %bitcast.141, f32[256,2,64,64]{3,2,1,0:T(8,128)} %fusion.183), kind=kCustom, calls=%fused_computation.2.clone.1 | custom fusion | flops 2097152 | bytes 25166848 | tf_op jit(solution)/shard_map/while/body/eval_jaxpr/scatter-add | solution.py:125
  396.4 29.5 %copy.85 = f32[4,128,2,64,64]{1,3,0,4,2:T(8,128)} copy(f32[4,128,2,64,64]{4,3,2,1,0:T(8,128)} %bitcast.124) | data formatting | bytes 33554432 | tf_op jit(solution)/shard_map/reshape | solution.py:129
  460.8 18.5 %fusion.8 = (f32[256,128,64]{1,0,2:T(8,128)}, f32[256,128,64]{1,0,2:T(8,128)}) fusion(f32[128,64]{0,1:T(8,128)S(1)} %copy-done.6, f32[128,64]{0,1:T(8,128)S(1)} %copy-done.7, f32[256,64,128]{2,0,1:T(8,128)} %fusion.51, f32[256,64,128]{2,0,1:T(8,128)} %fusion.59, f32[256,64,128]{2,0,1:T(8,128)} %fusion.53, f32[256,128,64]{1,0,2:T(8,128)} %bitcast.128), kind=kOutput, calls=%fused_computation.29 | convolution fusion | flops 3238232064 | bytes 50397184 | tf_op jit(solution)/shard_map/kq,rqp->rkp/dot_general | solution.py:16
  479.3 15.6 %fusion.28 = f32[64,256,128]{2,0,1:T(8,128)S(1)} fusion(f32[256,128,64]{1,0,2:T(8,128)} %get-tuple-element.119), kind=kOutput, calls=%fused_computation.57 | convolution fusion | flops 1610670080 | bytes 16777216 | tf_op jit(solution)/shard_map/rkp,pb->rbk/dot_general | solution.py:16
  494.9 17.3 %fusion.26 = f32[64,256,128]{2,0,1:T(8,128)} fusion(f32[256,128,64]{1,0,2:T(8,128)S(1)} %copy-done.2), kind=kOutput, calls=%fused_computation.55 | convolution fusion | flops 1610670080 | bytes 16777216 | tf_op jit(solution)/shard_map/rkp,pb->rbk/dot_general | solution.py:16
  512.2 17.5 %subtract_bitcast_fusion = f32[256,64,128]{2,1,0:T(8,128)} fusion(f32[64,256,128]{2,0,1:T(8,128)S(1)} %fusion.28, f32[256,128,64]{1,0,2:T(8,128)S(1)} %bitcast.130), kind=kOutput, calls=%fused_computation.38 | convolution fusion | flops 1612767232 | bytes 25165824 | tf_op jit(solution)/shard_map/rkp,pb->rbk/dot_general | solution.py:16
  539.1 18.0 %copy.90 = f32[1,256,8192]{1,0,2:T(1,128)} copy(f32[1,256,8192]{2,1,0:T(8,128)} %stack_reshape.6) | data formatting | bytes 16777216 | tf_op jit(solution)/shard_map/stack;reshape | solution.py:47
  557.1 18.9 %add_bitcast_fusion = f32[256,64,128]{2,1,0:T(8,128)} fusion(f32[64,256,128]{2,0,1:T(8,128)} %fusion.26, f32[256,128,64]{1,0,2:T(8,128)} %get-tuple-element.118), kind=kOutput, calls=%fused_computation.37 | convolution fusion | flops 1612767232 | bytes 25165824 | tf_op jit(solution)/shard_map/rkp,pb->rbk/dot_general | solution.py:16
  585.3 18.1 %copy.91 = f32[1,256,8192]{1,0,2:T(1,128)} copy(f32[1,256,8192]{2,1,0:T(8,128)} %stack_reshape.7) | data formatting | bytes 16777216 | tf_op jit(solution)/shard_map/stack;reshape | solution.py:47
  603.4 16.7 %pad_maximum_fusion = f32[2,256,8192]{1,0,2:T(2,128)S(1)} fusion(f32[1,256,8192]{1,0,2:T(1,128)} %copy.91, f32[1,256,8192]{1,0,2:T(1,128)} %copy.90), kind=kLoop, calls=%fused_computation.25 | loop fusion | flops 4194304 | bytes 33554432 | tf_op jit(solution)/shard_map/stack | solution.py:47
  620.1 371.7 %all_to_all.25 = f32[2,256,8192]{1,0,2:T(2,128)S(1)} all-to-all(f32[2,256,8192]{1,0,2:T(2,128)S(1)} %pad_maximum_fusion), channel_id=1, replica_groups=mesh['grp'=4,'dev'=8] {'grp','dev'}, dimensions={2} | all-to-all | bytes 33554432 | tf_op jit(solution)/shard_map/all_to_all | solution.py:132
  1012.9 17.5 %fusion.22 = f32[128,64,256]{2,0,1:T(8,128)} fusion(f32[128,64,256]{2,1,0:T(8,128)} %bitcast.131), kind=kOutput, calls=%fused_computation.51 | convolution fusion | flops 3221454848 | bytes 16777216 | tf_op jit(solution)/shard_map/bk,kpa->bpa/dot_general | solution.py:16
  1052.7 17.8 %fusion.20 = f32[128,64,256]{2,0,1:T(8,128)} fusion(f32[128,64,256]{2,1,0:T(8,128)} %bitcast.133), kind=kOutput, calls=%fused_computation.49 | convolution fusion | flops 3221454848 | bytes 16777216 | tf_op jit(solution)/shard_map/bk,kpa->bpa/dot_general | solution.py:16
  1070.6 20.2 %multiply_subtract_fusion = (f32[128,64,256]{2,0,1:T(8,128)S(1)}, f32[128,64,256]{2,0,1:T(8,128)S(1)}) fusion(f32[128,64]{0,1:T(8,128)S(1)} %copy-done.6, f32[128,64]{0,1:T(8,128)S(1)} %copy-done.7, f32[128,64,256]{2,0,1:T(8,128)} %fusion.22, f32[128,64,256]{2,0,1:T(8,128)} %fusion.24, f32[128,64,256]{2,0,1:T(8,128)} %fusion.20, f32[128,64,256]{2,1,0:T(8,128)} %bitcast.134), kind=kOutput, calls=%fused_computation.36 | convolution fusion | flops 3238232064 | bytes 50397184 | tf_op jit(solution)/shard_map/bk,kpa->bpa/dot_general | solution.py:16
  1090.8 13.4 %fusion.12 = f32[64,128,256]{2,0,1:T(8,128)} fusion(f32[128,64,256]{2,0,1:T(8,128)S(1)} %get-tuple-element.117), kind=kOutput, calls=%fused_computation.41 | convolution fusion | flops 1610670080 | bytes 16777216 | tf_op jit(solution)/shard_map/kpa,pb->abk/dot_general | solution.py:16
  1117.3 15.9 %multiply_bitcast_fusion.1 = f32[256,64,128]{0,1,2:T(8,128)} fusion(f32[64,128,256]{2,0,1:T(8,128)} %fusion.12, f32[128,64,256]{2,0,1:T(8,128)S(1)} %get-tuple-element.116), kind=kOutput, calls=%fused_computation.34 | convolution fusion | flops 1614864384 | bytes 25165824 | tf_op jit(solution)/shard_map/kpa,pb->abk/dot_general | solution.py:16
  1144.8 14.1 %multiply_bitcast_fusion = f32[256,64,128]{0,1,2:T(8,128)} fusion(f32[64,128,256]{2,0,1:T(8,128)S(1)} %copy-done.3, f32[128,64,256]{2,0,1:T(8,128)S(1)} %get-tuple-element.116), kind=kOutput, calls=%fused_computation.33 | convolution fusion | flops 1614864384 | bytes 25165824 | tf_op jit(solution)/shard_map/kpa,pb->abk/dot_general | solution.py:16
  1173.3 17.5 %copy.105 = f32[2,256,8192]{2,1,0:T(8,128)} copy(f32[2,256,8192]{1,2,0:T(8,128)} %pad_maximum_fusion.1) | data formatting | bytes 33554432 | tf_op jit(solution)/shard_map/stack | solution.py:69
  (107 shorter events, 258.5 us)
Async XLA Ops:
  7.2 58.0 %all-to-all-start = ((s32[32,32,3]{1,2,0:T(4,128)}), s32[32,32,3]{1,2,0:T(4,128)S(1)}, u32[]{:S(2)}, u32[]{:S(2)}) async-start(s32[32,32,3]{1,2,0:T(4,128)} %copy.83), calls=%async_computation | async-start | bytes 131072 | tf_op jit(solution)/shard_map/all_to_all | solution.py:96
  65.2 22.7 %all-to-all-start.1 = ((bf16[32,32,2,128]{3,2,1,0:T(2,128)(2,1)}), bf16[32,32,2,128]{3,2,1,0:T(2,128)(2,1)S(1)}, u32[]{:S(2)}, u32[]{:S(2)}) async-start(bf16[32,32,2,128]{3,2,1,0:T(2,128)(2,1)} %bitcast.16), calls=%async_computation.1 | async-start | bytes 1048576 | tf_op jit(solution)/shard_map/all_to_all | solution.py:89
  87.9 11.3 copy-start.5
  432.6 18.9 %copy-start = (f32[1,4,64,128,64]{3,2,1,4,0:T(8,128)}, f32[1,4,64,128,64]{3,2,1,4,0:T(8,128)S(1)}, u32[]{:S(2)}) copy-start(f32[1,4,64,128,64]{3,2,1,4,0:T(8,128)S(1)} %get-tuple-element.123) | copy-start | bytes 25165828
  451.5 9.3 copy-start.6
  451.5 9.3 copy-start.7
  479.3 15.7 %copy-start.2 = (f32[256,128,64]{1,0,2:T(8,128)S(1)}, f32[256,128,64]{1,0,2:T(8,128)}, u32[]{:S(2)}) copy-start(f32[256,128,64]{1,0,2:T(8,128)} %get-tuple-element.119) | copy-start | bytes 25165828
  479.3 32.9 %slice-start = ((s8[8388608]{0:T(1024)(128)(4,1)}), s8[4194304]{0:T(1024)(128)(4,1)S(1)}, s32[]{:S(2)}) async-start(s8[8388608]{0:T(1024)(128)(4,1)} %bitcast.129), calls=%async_computation.3 | async-start | bytes 8388608
  494.9 17.3 %slice-start.1 = ((s8[8388608]{0:T(1024)(128)(4,1)}), s8[4194304]{0:T(1024)(128)(4,1)S(1)}, s32[]{:S(2)}) async-start(s8[8388608]{0:T(1024)(128)(4,1)} %bitcast.129), calls=%async_computation.4 | async-start | bytes 8388608
  1012.9 17.5 %copy-start.1 = (f32[1,32,256,256]{3,2,1,0:T(8,128)S(1)}, f32[1,32,256,256]{3,2,1,0:T(8,128)}, u32[]{:S(2)}) copy-start(f32[1,32,256,256]{3,2,1,0:T(8,128)} %copy.93) | copy-start | bytes 25165828
  1133.2 11.6 copy-start.3
  1158.9 8.4 copy-start.4
where the time goes:
time: 1200 us; the launch traced here: 1190 us
  blocking collectives  372 us (31%)
  matrix products  283 us (24%)
  other arithmetic  258 us (22%)
  local copies, waits for them, and re-layouts  248 us (21%)
  waiting for transfers between devices  15.5 us (1%)
  starting transfers between devices  13.7 us (1%)
    all_to_all x1, blocking collectives, local(): lax.all_to_all(half, ('grp', 'dev'), split_axis=2, concat_axis=1, tiled=T...  372 us
    dot_general x16, matrix products, product(): return jnp.einsum(pattern, first, second, precision=lax.Precision.HIGHEST)  241 us
    scatter-add x4, other arithmetic, grid_block(): return uv_tiles.at[label_block[:, 0]].add(terms)  209 us
    another operation x4, local copies, waits for them, and re-layouts, along_rows(): jnp.stack([result_re.reshape(lines, GRID), result_im.reshape(lines, GRID)])  54.8 us
    scatter x1, local copies, waits for them, and re-layouts, local(): jnp.zeros((total_rows, 2, VIS), jnp.bfloat16).at[position].set(visibilities)  49.6 us
    dot_general x4, matrix products, grid_block(): jnp.einsum('rcik,rjk->rcij', weighted, right_kernel, preferred_element_ty...  41.5 us
    reshape x1, local copies, waits for them, and re-layouts, local(): uv_tiles.reshape(tile_rows, tile_cols, 2, TILE, TILE)  29.5 us
  transfers between devices with their start and end apart: 2, of which 1 were waited for; matrix products, arithmetic and copies ran while one was open for 4% of the time, Pallas kernels for 0%

commit v1 on v0

--- a/solution.py
+++ b/solution.py
@@ -129,7 +129,11 @@
     grid_rows = uv_tiles.reshape(tile_rows, tile_cols, 2, TILE, TILE).transpose(2, 0, 3, 1, 4)
     grid_rows = grid_rows.reshape(2, slab, GRID)
     half = along_rows(grid_rows)
-    columns = lax.all_to_all(half, ("grp", "dev"), split_axis=2, concat_axis=1, tiled=True)
+    lower = jax.lax.axis_size(("grp", "dev"))
+    frame_out = jnp.split(half, lower, axis=2)
+    a_next = jnp.stack(frame_out)
+    view_out = jax.lax.all_to_all(a_next, ("grp", "dev"), 0, 0)
+    columns = jnp.concatenate(view_out, axis=1)
     source_order = jnp.arange(QLEN, dtype=jnp.int32)
     return along_columns(columns, source_order)
 

time: 1200 us -> 1160 us (0.967)
  local copies, waits for them, and re-layouts: 248 us -> 230 us
  other arithmetic: 258 us -> 242 us
    another operation x4 -> x3, local copies, waits for them, and re-layouts: 54.8 us -> 22.7 us  [along_rows(): jnp.stack([result_re.reshape(lines, GRID), result_im.reshape(lines, GRID)])]
    unnamed x20 -> x52, local copies, waits for them, and re-layouts: 0.04 us -> 29.8 us
    another operation x3 -> x2, other arithmetic: 17.9 us -> 1.19 us  [the longest x1 16.7 us: along_rows(): jnp.stack([result_re.reshape(lines, GRID), result_im.reshape(lines, GRID)])]
where the time goes in v1:
time: 1160 us; the launch traced here: 1150 us
  blocking collectives  372 us (32%)
  matrix products  274 us (24%)
  other arithmetic  242 us (21%)
  local copies, waits for them, and re-layouts  230 us (20%)
  waiting for transfers between devices  15.5 us (1%)
  starting transfers between devices  13.7 us (1%)
    all_to_all x1, blocking collectives, local(): view_out = jax.lax.all_to_all(a_next, ('grp', 'dev'), 0, 0)  372 us
    dot_general x16, matrix products, product(): return jnp.einsum(pattern, first, second, precision=lax.Precision.HIGHEST)  233 us
    scatter-add x4, other arithmetic, grid_block(): return uv_tiles.at[label_block[:, 0]].add(terms)  209 us
    scatter x1, local copies, waits for them, and re-layouts, local(): jnp.zeros((total_rows, 2, VIS), jnp.bfloat16).at[position].set(visibilities)  49.6 us
    dot_general x4, matrix products, grid_block(): jnp.einsum('rcik,rjk->rcij', weighted, right_kernel, preferred_element_ty...  41.5 us
    unnamed x52, local copies, waits for them, and re-layouts  29.8 us
    reshape x1, local copies, waits for them, and re-layouts, local(): uv_tiles.reshape(tile_rows, tile_cols, 2, TILE, TILE)  29.5 us
  transfers between devices with their start and end apart: 2, of which 1 were waited for; matrix products, arithmetic and copies ran while one was open for 4% of the time, Pallas kernels for 0%

profile of v1, /device:TPU:0, one launch (start us, length us, event | category | flops | bytes accessed | tf_op | source)
XLA Modules:
  0.0 1147.6 jit_solution(7824735748559662606)
XLA Ops:
  15.5 49.6 %scatter_fusion.1 = bf16[1024,2,128]{2,1,0:T(2,128)(2,1)} fusion(bf16[1024,2,128]{2,1,0:T(2,128)(2,1)} %broadcast_in_dim.29, s32[512]{0:T(512)S(1)} %bitcast.277, bf16[512,2,128]{2,1,0:T(2,128)(2,1)} %param.9), kind=kCustom, calls=%fused_computation.4 | custom fusion | bytes 788480 | tf_op jit(solution)/shard_map/scatter | solution.py:85
  72.4 15.5 %all-to-all-done.1 = bf16[32,32,2,128]{3,2,1,0:T(2,128)(2,1)S(1)} async-done(((bf16[32,32,2,128]{3,2,1,0:T(2,128)(2,1)}), bf16[32,32,2,128]{3,2,1,0:T(2,128)(2,1)S(1)}, u32[]{:S(2)}, u32[]{:S(2)}) %all-to-all-start.1) | async-done | bytes 524320 | tf_op jit(solution)/shard_map/all_to_all | solution.py:89
  99.1 297.3 %while.13 = (s32[]{:T(128)}, f32[512,2,64,64]{3,2,1,0:T(8,128)}, s32[1024,3]{0,1:T(4,128)S(1)}, bf16[2,32,64,128]{3,2,1,0:T(8,128)(2,1)S(1)}, bf16[1024,2,128]{2...) while((s32[]{:T(128)}, f32[512,2,64,64]{3,2,1,0:T(8,128)}, ...), condition=%wide.region_7.9_spmd, body=%wide.region_5.0_spmd.sunk | while | flops 553721088 | bytes 78276800 | solution.py:128
  121.2 52.2 %scatter_fusion = f32[512,2,64,64]{3,2,1,0:T(8,128)} fusion(f32[512,2,64,64]{3,2,1,0:T(8,128)} %get-tuple-element.179, s32[256]{0:T(256)S(1)} %bitcast.269, f32[256,2,64,64]{3,2,1,0:T(8,128)} %fusion.215), kind=kCustom, calls=%fused_computation.2.clone.1 | custom fusion | flops 2097152 | bytes 25166848 | tf_op jit(solution)/shard_map/while/body/eval_jaxpr/scatter-add | solution.py:125
  195.5 52.3 %scatter_fusion = f32[512,2,64,64]{3,2,1,0:T(8,128)} fusion(f32[512,2,64,64]{3,2,1,0:T(8,128)} %get-tuple-element.179, s32[256]{0:T(256)S(1)} %bitcast.269, f32[256,2,64,64]{3,2,1,0:T(8,128)} %fusion.215), kind=kCustom, calls=%fused_computation.2.clone.1 | custom fusion | flops 2097152 | bytes 25166848 | tf_op jit(solution)/shard_map/while/body/eval_jaxpr/scatter-add | solution.py:125
  269.9 52.2 %scatter_fusion = f32[512,2,64,64]{3,2,1,0:T(8,128)} fusion(f32[512,2,64,64]{3,2,1,0:T(8,128)} %get-tuple-element.179, s32[256]{0:T(256)S(1)} %bitcast.269, f32[256,2,64,64]{3,2,1,0:T(8,128)} %fusion.215), kind=kCustom, calls=%fused_computation.2.clone.1 | custom fusion | flops 2097152 | bytes 25166848 | tf_op jit(solution)/shard_map/while/body/eval_jaxpr/scatter-add | solution.py:125
  344.1 52.3 %scatter_fusion = f32[512,2,64,64]{3,2,1,0:T(8,128)} fusion(f32[512,2,64,64]{3,2,1,0:T(8,128)} %get-tuple-element.179, s32[256]{0:T(256)S(1)} %bitcast.269, f32[256,2,64,64]{3,2,1,0:T(8,128)} %fusion.215), kind=kCustom, calls=%fused_computation.2.clone.1 | custom fusion | flops 2097152 | bytes 25166848 | tf_op jit(solution)/shard_map/while/body/eval_jaxpr/scatter-add | solution.py:125
  396.4 29.5 %copy.89 = f32[4,128,2,64,64]{1,3,0,4,2:T(8,128)} copy(f32[4,128,2,64,64]{4,3,2,1,0:T(8,128)} %bitcast.252) | data formatting | bytes 33554432 | tf_op jit(solution)/shard_map/reshape | solution.py:129
  460.8 18.5 %fusion.8 = (f32[256,128,64]{1,0,2:T(8,128)}, f32[256,128,64]{1,0,2:T(8,128)}) fusion(f32[128,64]{0,1:T(8,128)S(1)} %copy-done.6, f32[128,64]{0,1:T(8,128)S(1)} %copy-done.7, f32[256,64,128]{2,0,1:T(8,128)} %fusion.83, f32[256,64,128]{2,0,1:T(8,128)} %fusion.91, f32[256,64,128]{2,0,1:T(8,128)} %fusion.85, f32[256,128,64]{1,0,2:T(8,128)} %bitcast.256), kind=kOutput, calls=%fused_computation.29 | convolution fusion | flops 3238232064 | bytes 50397184 | tf_op jit(solution)/shard_map/kq,rqp->rkp/dot_general | solution.py:16
  479.3 15.7 %fusion.26 = f32[64,256,128]{2,0,1:T(8,128)S(1)} fusion(f32[256,128,64]{1,0,2:T(8,128)} %get-tuple-element.119), kind=kOutput, calls=%fused_computation.55 | convolution fusion | flops 1610670080 | bytes 16777216 | tf_op jit(solution)/shard_map/rkp,pb->rbk/dot_general | solution.py:16
  495.0 17.2 %fusion.28 = f32[64,256,128]{2,0,1:T(8,128)} fusion(f32[256,128,64]{1,0,2:T(8,128)S(1)} %copy-done.1), kind=kOutput, calls=%fused_computation.57 | convolution fusion | flops 1610670080 | bytes 16777216 | tf_op jit(solution)/shard_map/rkp,pb->rbk/dot_general | solution.py:16
  512.2 17.5 %add_bitcast_fusion = f32[256,64,128]{2,1,0:T(8,128)} fusion(f32[64,256,128]{2,0,1:T(8,128)S(1)} %fusion.26, f32[256,128,64]{1,0,2:T(8,128)S(1)} %bitcast.258), kind=kOutput, calls=%fused_computation.37 | convolution fusion | flops 1612767232 | bytes 25165824 | tf_op jit(solution)/shard_map/rkp,pb->rbk/dot_general | solution.py:16
  539.1 18.9 %subtract_bitcast_fusion = f32[256,64,128]{2,1,0:T(8,128)} fusion(f32[64,256,128]{2,0,1:T(8,128)} %fusion.28, f32[256,128,64]{1,0,2:T(8,128)} %get-tuple-element.118), kind=kOutput, calls=%fused_computation.38 | convolution fusion | flops 1612767232 | bytes 25165824 | tf_op jit(solution)/shard_map/rkp,pb->rbk/dot_general | solution.py:16
  602.0 371.9 %all_to_all.15 = f32[32,2,256,256]{3,2,1,0:T(8,128)S(1)} all-to-all(f32[32,2,256,256]{3,2,1,0:T(8,128)} %fusion.42), channel_id=1, replica_groups=mesh['grp'=4,'dev'=8] {'grp','dev'}, dimensions={0} | all-to-all | bytes 33554432 | tf_op jit(solution)/shard_map/all_to_all | solution.py:135
  986.8 13.1 %fusion.22 = f32[128,64,256]{2,0,1:T(8,128)} fusion(f32[128,64,256]{2,1,0:T(8,128)S(1)} %bitcast.259), kind=kOutput, calls=%fused_computation.51 | convolution fusion | flops 3221454848 | bytes 16777216 | tf_op jit(solution)/shard_map/bk,kpa->bpa/dot_general | solution.py:16
  999.9 13.5 %fusion.24 = f32[128,64,256]{2,0,1:T(8,128)} fusion(f32[128,64,256]{2,1,0:T(8,128)S(1)} %bitcast.260), kind=kOutput, calls=%fused_computation.53 | convolution fusion | flops 3221454848 | bytes 16777216 | tf_op jit(solution)/shard_map/bk,kpa->bpa/dot_general | solution.py:16
  1013.4 13.1 %fusion.20 = f32[128,64,256]{2,0,1:T(8,128)} fusion(f32[128,64,256]{2,1,0:T(8,128)S(1)} %bitcast.261), kind=kOutput, calls=%fused_computation.49 | convolution fusion | flops 3221454848 | bytes 16777216 | tf_op jit(solution)/shard_map/bk,kpa->bpa/dot_general | solution.py:16
  1026.6 20.4 %multiply_subtract_fusion = (f32[128,64,256]{2,0,1:T(8,128)S(1)}, f32[128,64,256]{2,0,1:T(8,128)S(1)}) fusion(f32[128,64]{0,1:T(8,128)S(1)} %copy-done.6, f32[128,64]{0,1:T(8,128)S(1)} %copy-done.7, f32[128,64,256]{2,0,1:T(8,128)} %fusion.22, f32[128,64,256]{2,0,1:T(8,128)} %fusion.24, f32[128,64,256]{2,0,1:T(8,128)} %fusion.20, f32[128,64,256]{2,1,0:T(8,128)} %bitcast.262), kind=kOutput, calls=%fused_computation.36 | convolution fusion | flops 3238232064 | bytes 50397184 | tf_op jit(solution)/shard_map/bk,kpa->bpa/dot_general | solution.py:16
  1046.9 13.2 %fusion.12 = f32[64,128,256]{2,0,1:T(8,128)} fusion(f32[128,64,256]{2,0,1:T(8,128)S(1)} %get-tuple-element.117), kind=kOutput, calls=%fused_computation.41 | convolution fusion | flops 1610670080 | bytes 16777216 | tf_op jit(solution)/shard_map/kpa,pb->abk/dot_general | solution.py:16
  1060.1 13.4 %fusion.10 = f32[64,128,256]{2,0,1:T(8,128)} fusion(f32[128,64,256]{2,0,1:T(8,128)S(1)} %get-tuple-element.117), kind=kOutput, calls=%fused_computation.39 | convolution fusion | flops 1610670080 | bytes 16777216 | tf_op jit(solution)/shard_map/kpa,pb->abk/dot_general | solution.py:16
  1073.5 15.9 %multiply_bitcast_fusion.1 = f32[256,64,128]{0,1,2:T(8,128)} fusion(f32[64,128,256]{2,0,1:T(8,128)} %fusion.12, f32[128,64,256]{2,0,1:T(8,128)S(1)} %get-tuple-element.116), kind=kOutput, calls=%fused_computation.34 | convolution fusion | flops 1614864384 | bytes 25165824 | tf_op jit(solution)/shard_map/kpa,pb->abk/dot_general | solution.py:16
  1089.4 11.6 %copy.101 = f32[256,64,128]{0,2,1:T(8,128)} copy(f32[256,64,128]{0,1,2:T(8,128)} %multiply_bitcast_fusion.1) | data formatting | bytes 16777216 | tf_op jit(solution)/shard_map/mul | solution.py:70
  1101.1 14.1 %multiply_bitcast_fusion = f32[256,64,128]{0,1,2:T(8,128)} fusion(f32[64,128,256]{2,0,1:T(8,128)S(1)} %copy-done.3, f32[128,64,256]{2,0,1:T(8,128)S(1)} %get-tuple-element.116), kind=kOutput, calls=%fused_computation.33 | convolution fusion | flops 1614864384 | bytes 25165824 | tf_op jit(solution)/shard_map/kpa,pb->abk/dot_general | solution.py:16
  1129.6 17.5 %copy.105 = f32[2,256,8192]{2,1,0:T(8,128)} copy(f32[2,256,8192]{1,2,0:T(8,128)} %pad_maximum_fusion) | data formatting | bytes 33554432 | tf_op jit(solution)/shard_map/stack | solution.py:69
  (136 shorter events, 237.8 us)
Async XLA Ops:
  7.2 58.0 %all-to-all-start = ((s32[32,32,3]{1,2,0:T(4,128)}), s32[32,32,3]{1,2,0:T(4,128)S(1)}, u32[]{:S(2)}, u32[]{:S(2)}) async-start(s32[32,32,3]{1,2,0:T(4,128)} %copy.87), calls=%async_computation | async-start | bytes 131072 | tf_op jit(solution)/shard_map/all_to_all | solution.py:96
  65.2 22.7 %all-to-all-start.1 = ((bf16[32,32,2,128]{3,2,1,0:T(2,128)(2,1)}), bf16[32,32,2,128]{3,2,1,0:T(2,128)(2,1)S(1)}, u32[]{:S(2)}, u32[]{:S(2)}) async-start(bf16[32,32,2,128]{3,2,1,0:T(2,128)(2,1)} %bitcast.16), calls=%async_computation.1 | async-start | bytes 1048576 | tf_op jit(solution)/shard_map/all_to_all | solution.py:89
  87.9 11.3 copy-start.5
  432.6 18.9 %copy-start = (f32[1,4,64,128,64]{3,2,1,4,0:T(8,128)}, f32[1,4,64,128,64]{3,2,1,4,0:T(8,128)S(1)}, u32[]{:S(2)}) copy-start(f32[1,4,64,128,64]{3,2,1,4,0:T(8,128)S(1)} %get-tuple-element.123) | copy-start | bytes 25165828
  451.5 9.3 copy-start.6
  451.5 9.3 copy-start.7
  479.3 15.7 %copy-start.1 = (f32[256,128,64]{1,0,2:T(8,128)S(1)}, f32[256,128,64]{1,0,2:T(8,128)}, u32[]{:S(2)}) copy-start(f32[256,128,64]{1,0,2:T(8,128)} %get-tuple-element.119) | copy-start | bytes 25165828
  479.3 33.0 %slice-start = ((s8[8388608]{0:T(1024)(128)(4,1)}), s8[4194304]{0:T(1024)(128)(4,1)S(1)}, s32[]{:S(2)}) async-start(s8[8388608]{0:T(1024)(128)(4,1)} %bitcast.257), calls=%async_computation.3 | async-start | bytes 8388608
  495.0 17.3 %slice-start.1 = ((s8[8388608]{0:T(1024)(128)(4,1)}), s8[4194304]{0:T(1024)(128)(4,1)S(1)}, s32[]{:S(2)}) async-start(s8[8388608]{0:T(1024)(128)(4,1)} %bitcast.257), calls=%async_computation.4 | async-start | bytes 8388608
  986.8 26.6 %copy-start.2 = (f32[1,32,256,256]{3,2,1,0:T(8,128)}, f32[1,32,256,256]{3,2,1,0:T(8,128)S(1)}, u32[]{:S(2)}) copy-start(f32[1,32,256,256]{3,2,1,0:T(8,128)S(1)} %get-tuple-element.121) | copy-start | bytes 25165828
  1089.4 11.6 %copy-start.3 = (f32[64,128,256]{2,0,1:T(8,128)S(1)}, f32[64,128,256]{2,0,1:T(8,128)}, u32[]{:S(2)}) copy-start(f32[64,128,256]{2,0,1:T(8,128)} %fusion.10) | copy-start | bytes 25165828
  1115.2 8.4 copy-start.4
